TPU v7x, 768 devices: a whole 4x8x12 slice. The times are simulated.
768 devices in a mesh: lat: 32 (over y_lo, x, core), lon: 24 (over y_hi, z).
Axes of the slice: x: 4, y: 8 (y_hi: 2, y_lo: 4; y = y_hi * 4 + y_lo), z: 12, core: 2. Of those that a mesh axis runs over, the one named last changes fastest.
Arguments:
- tokens: bfloat16 [256, 384, 1024], P('lat', 'lon'), may hold values from -300 to 300, as said below
- w_qkv: bfloat16 [1024, 3072], P(None, 'lon'), may hold values from -0.1875 to 0.1875
- rel_bias: float32 [16, 13, 13], replicated, may hold values from -4 to 4
- tile_valid: int32 [32, 48, 9], P('lat', 'lon'), may hold values 0 or 1
Outputs:
- context: bfloat16 [256, 384, 1024], P('lat', 'lon')
Inputs may be any that keep to these rules, and one draw needn't show every extreme that they name: `tokens`: token features are finite real values; most are of order one.
All inputs are finite; a program needn't handle non-finite values. No bound on the sum of `tile_valid` on one device may be relied on, other than what follows from the above.
Results may differ from a plain program's by a relative error of at most 0.012.
The roundings to bfloat16 on the way count: a program that leaves them out, or rounds other values in their place, can miss the bound.
Values may be sent and summed in bfloat16 or wider, within the bound.
A program may use at most 64 MiB of HBM per device.

v0:
```python
import math

import jax
import jax.numpy as jnp
import numpy as np
from jax import lax
from jax.sharding import PartitionSpec as P

HEADS = 16
HD = 64
TILE = 8
RADIUS = 6


def padded(cells, sides, width, closed):
    for axis, dim in sides:
        count = lax.axis_size(axis)
        ends = count if closed else count - 1
        head = lax.slice_in_dim(cells, 0, width, axis=dim)
        tail = lax.slice_in_dim(cells, cells.shape[dim] - width, cells.shape[dim], axis=dim)
        cells = jnp.concatenate(
            [
                lax.ppermute(tail, axis, [(i, (i + 1) % count) for i in range(ends)]),
                cells,
                lax.ppermute(head, axis, [((i + 1) % count, i) for i in range(ends)]),
            ],
            axis=dim,
        )
    return cells


def static_tables():
    side = TILE + 2 * RADIUS
    qrow = np.repeat(np.arange(TILE), TILE)
    qcol = np.tile(np.arange(TILE), TILE)
    krow = np.repeat(np.arange(side), side) - RADIUS
    kcol = np.tile(np.arange(side), side) - RADIUS
    off_r = krow[None, :] - qrow[:, None]
    off_c = kcol[None, :] - qcol[:, None]
    inside = (np.abs(off_r) <= RADIUS) & (np.abs(off_c) <= RADIUS)
    slot = 3 * (krow // TILE + 1) + (kcol // TILE + 1)
    onehot = (slot[:, None] == np.arange(9)[None, :]).astype(np.float32)
    idx_r = np.clip(off_r, -RADIUS, RADIUS) + RADIUS
    idx_c = np.clip(off_c, -RADIUS, RADIUS) + RADIUS
    return (inside, slot, onehot, idx_r, idx_c, krow)


def tile_attend(q_tile, k_tile, v_tile, bias, inside, slot, onehot, flags, row_ok):
    scores = jnp.einsum("qhd,khd->hqk", q_tile, k_tile, preferred_element_type=jnp.float32)
    scores = scores * (1.0 / math.sqrt(HD)) + bias
    flag_key = (jnp.dot(jnp.asarray(onehot), flags.astype(jnp.float32)) > 0.5) | jnp.asarray(
        slot == 4
    )
    mask = jnp.asarray(inside) & flag_key[None, :] & row_ok[None, :]
    scores = jnp.where(mask[None], scores, -1e30)
    top = jnp.max(scores, axis=2, keepdims=True)
    expo = jnp.where(mask[None], jnp.exp(scores - top), 0.0)
    total = jnp.sum(expo, axis=2, keepdims=True)
    weight = (expo / total).astype(jnp.bfloat16)
    return jnp.einsum("hqk,khd->qhd", weight, v_tile, preferred_element_type=jnp.float32).astype(
        jnp.bfloat16
    )


def per_device(tokens, w_qkv, rel_bias, tile_valid):
    rows, cols, width = tokens.shape
    inside, slot, onehot, idx_r, idx_c, krow = static_tables()
    side = TILE + 2 * RADIUS
    flat = tokens.reshape(rows * cols, width)
    qkv = (
        jnp.dot(
            flat,
            lax.all_gather(w_qkv, "lon", axis=1, tiled=True),
            preferred_element_type=jnp.float32,
        )
        .astype(jnp.bfloat16)
        .reshape(rows, cols, 3 * width)
    )
    query = qkv[:, :, :width]
    keyval = qkv[:, :, width:]
    keyval = padded(keyval, (("lat", 0),), RADIUS, False)
    keyval = padded(keyval, (("lon", 1),), RADIUS, True)
    bias = rel_bias[:, idx_r, idx_c]
    total_rows = rows * lax.axis_size("lat")
    row_base = lax.axis_index("lat") * rows
    tiles_c = cols // TILE
    ids = jnp.arange(rows // TILE * tiles_c, dtype=jnp.int32)

    def one_tile(tid):
        trow = tid // tiles_c
        tcol = tid % tiles_c
        q_tile = lax.dynamic_slice(
            query, (trow * TILE, tcol * TILE, jnp.int32(0)), (TILE, TILE, width)
        )
        region = lax.dynamic_slice(
            keyval, (trow * TILE, tcol * TILE, jnp.int32(0)), (side, side, 2 * width)
        )
        region = region.reshape(side * side, 2 * width)
        k_tile = region[:, :width].reshape(side * side, HEADS, width // HEADS)
        v_tile = region[:, width:].reshape(side * side, HEADS, width // HEADS)
        grow = row_base + trow * TILE + jnp.asarray(krow, dtype=jnp.int32)
        row_ok = (grow >= 0) & (grow < total_rows)
        flags = tile_valid[trow, tcol]
        out = tile_attend(
            q_tile.reshape(TILE * TILE, HEADS, width // HEADS),
            k_tile,
            v_tile,
            bias,
            inside,
            slot,
            onehot,
            flags,
            row_ok,
        )
        return out.reshape(TILE, TILE, width)

    result = lax.map(one_tile, ids)
    result = result.reshape(rows // TILE, tiles_c, TILE, TILE, width).transpose(0, 2, 1, 3, 4)
    return result.reshape(rows, cols, width)


def solution(mesh):
    placed = (P("lat", "lon", None), P(None, "lon"), P(), P("lat", "lon", None))
    return jax.shard_map(
        per_device, mesh=mesh, in_specs=placed, out_specs=P("lat", "lon", None), check_vma=False
    )
```

profile of v0, /device:TPU:7, one launch (start us, length us, event | category | flops | bytes accessed | tf_op | source)
XLA Modules:
  0.0 613.5 jit_solution(4576207540504620529)
XLA Ops:
  6.5 0.7 all-gather.2.cloned.1.call-update
  7.3 208.5 %all-gather.2.cloned.1.call-done = bf16[1024,3072]{1,0:T(8,128)(2,1)} async-done(((bf16[1024,128]{1,0:T(8,128)(2,1)}), bf16[1024,3072]{1,0:T(8,128)(2,1)}) %all-gather.2.cloned.1.call-update) | async-done | bytes 6291472 | tf_op jit(solution)/shard_map/all_gather | solution.py:73
  215.8 3.8 convolution_convert_fusion.1
  219.8 9.8 %collective-permute-start = (bf16[6,16,2048]{2,0,1:T(8,128)(2,1)S(1)}, bf16[6,16,2048]{2,0,1:T(8,128)(2,1)S(1)}, u32[]{:S(2)}, u32[]{:S(2)}) collective-permute-start(bf16[6,16,2048]{2,0,1:T(8,128)(2,1)S(1)} %copy.36), channel_id=1, source_target_pairs={{0,24},{24,48},{48,72},{72,96},{96,120},{120,144},{144,168},{168,1... | collective-permute-start | bytes 1179656 | tf_op jit(solution)/shard_map/ppermute | solution.py:23
  229.9 1.9 collective-permute-start.1
  232.2 3.6 collective-permute-done
  235.8 32.0 %collective-permute-done.1 = bf16[6,16,2048]{2,0,1:T(8,128)(2,1)S(1)} collective-permute-done((bf16[6,16,2048]{2,0,1:T(8,128)(2,1)S(1)}, bf16[6,16,2048]{2,0,1:T(8,128)(2,1)S(1)}, u32[]{:S(2)}, u32[]{:S(2)}) %collective-permute-start.1) | collective-permute-done | bytes 393248 | tf_op jit(solution)/shard_map/ppermute | solution.py:25
  267.8 1.5 pad_maximum_fusion.3
  269.3 1.9 collective-permute-start.2
  271.2 9.4 %collective-permute-start.3 = (bf16[20,6,2048]{2,0,1:T(8,128)(2,1)}, bf16[20,6,2048]{2,0,1:T(8,128)(2,1)}, u32[]{:S(2)}, u32[]{:S(2)}) collective-permute-start(bf16[20,6,2048]{2,0,1:T(8,128)(2,1)} %get-tuple-element.230), channel_id=1, source_target_pairs={{1,0},{2,1},{3,2},{4,3},{5,4},{6,5},{7,6},{8,7},{9,8},{10,9},{11,1... | collective-permute-start | bytes 1474568 | tf_op jit(solution)/shard_map/ppermute | solution.py:25
  280.8 276.4 %gather_fusion = f32[25600,16]{1,0:T(8,128)} fusion(f32[16,13,13]{0,2,1:T(8,128)S(1)} %copy.31, s32[25600]{0:T(1024)S(1)} %copy-done.1), kind=kCustom, calls=%fused_computation | custom fusion | bytes 3481600 | tf_op jit(solution)/shard_map/gather | solution.py:83
  557.2 10.2 %copy.32 = f32[64,400,16]{1,0,2:T(8,128)} copy(f32[64,400,16]{2,1,0:T(8,128)} %bitcast.48) | data formatting | bytes 3276800 | tf_op jit(solution)/shard_map/gather | solution.py:83
  567.4 0.7 slice.49
  568.1 2.2 pad_maximum_fusion
  570.4 34.6 %while.13 = (s32[]{:T(128)}, bf16[2,8,8,1024]{3,2,1,0:T(8,128)(2,1)}, s32[2]{0:T(128)S(1)}, bf16[20,28,2048]{2,0,1:T(8,128)(2,1)S(1)}, s32[1,2,9]{2,1,0:T(2,128)...) while((s32[]{:T(128)}, ...), condition=%wide.region_3.4_spmd.clone, body=%wide.region_0.3_spmd.sunk.clone.sunk | while | flops 108261176 | bytes 44236192 | solution.py:117
  570.4 0.7 dynamic_slice.51
  573.2 0.9 copy.50
  574.1 1.4 reshape.105
  575.5 1.6 fusion.34
  578.7 4.0 fusion.37
  582.7 1.3 copy.51
  584.0 2.6 fusion.38
  587.1 0.7 constant_dynamic-update-slice_fusion.2
  587.7 0.7 dynamic_slice.51
  590.5 0.9 copy.50
  591.4 1.4 reshape.105
  592.8 1.6 fusion.34
  596.1 3.9 fusion.37
  600.0 1.3 copy.51
  601.3 2.6 fusion.38
  604.4 0.7 constant_dynamic-update-slice_fusion.2
  605.0 1.7 copy_bitcast_fusion
  (65 shorter events, 4.1 us)
Async XLA Ops:
  6.5 209.2 %copy-start = (bf16[8,16,1024]{2,1,0:T(8,128)(2,1)S(1)}, bf16[8,16,1024]{2,1,0:T(8,128)(2,1)}, u32[]{:S(2)}) copy-start(bf16[8,16,1024]{2,1,0:T(8,128)(2,1)} %param.14) | copy-start | bytes 786436
  6.5 209.2 %all-gather.2.cloned.1.call-start = ((), (), s32[]{:S(2)}) async-start(), calls=%async_computation | async-start | bytes 6553600 | tf_op jit(solution)/shard_map/all_gather | solution.py:73
  219.8 15.9 %collective-permute-start = (bf16[6,16,2048]{2,0,1:T(8,128)(2,1)S(1)}, bf16[6,16,2048]{2,0,1:T(8,128)(2,1)S(1)}, u32[]{:S(2)}, u32[]{:S(2)}) collective-permute-start(bf16[6,16,2048]{2,0,1:T(8,128)(2,1)S(1)} %copy.36), channel_id=1, source_target_pairs={{0,24},{24,48},{48,72},{72,96},{96,120},{120,144},{144,168},{168,1... | collective-permute-start | bytes 1179656 | tf_op jit(solution)/shard_map/ppermute | solution.py:23
  229.9 37.9 %collective-permute-start.1 = (bf16[6,16,2048]{2,0,1:T(8,128)(2,1)S(1)}, bf16[6,16,2048]{2,0,1:T(8,128)(2,1)S(1)}, u32[]{:S(2)}, u32[]{:S(2)}) collective-permute-start(bf16[6,16,2048]{2,0,1:T(8,128)(2,1)S(1)} %copy.38), channel_id=1, source_target_pairs={{24,0},{48,24},{72,48},{96,72},{120,96},{144,120},{168,144},{192,1... | collective-permute-start | bytes 1179656 | tf_op jit(solution)/shard_map/ppermute | solution.py:25
  231.9 48.7 %copy-start.9 = (f32[16,13,13]{2,0,1:T(8,128)S(1)}, f32[16,13,13]{2,0,1:T(8,128)}, u32[]{:S(2)}) copy-start(f32[16,13,13]{2,0,1:T(8,128)} %param.16) | copy-start | bytes 32452
  231.9 48.9 %copy-start.1 = (s32[25600]{0:T(1024)S(1)}, s32[25600]{0:T(1024)}, u32[]{:S(2)}) copy-start(s32[25600]{0:T(1024)} %constant.162) | copy-start | bytes 307204
  235.8 321.4 %copy-start.6 = (bf16[6,16,2048]{2,0,1:T(8,128)(2,1)}, bf16[6,16,2048]{2,0,1:T(8,128)(2,1)S(1)}, u32[]{:S(2)}) copy-start(bf16[6,16,2048]{2,0,1:T(8,128)(2,1)S(1)} %collective-permute-done) | copy-start | bytes 1179652
  267.8 289.4 %copy-start.7 = (bf16[6,16,2048]{2,0,1:T(8,128)(2,1)}, bf16[6,16,2048]{2,0,1:T(8,128)(2,1)S(1)}, u32[]{:S(2)}) copy-start(bf16[6,16,2048]{2,0,1:T(8,128)(2,1)S(1)} %collective-permute-done.1) | copy-start | bytes 1179652
  269.3 298.8 %collective-permute-start.2 = (bf16[20,6,2048]{2,0,1:T(8,128)(2,1)}, bf16[20,6,2048]{2,0,1:T(8,128)(2,1)}, u32[]{:S(2)}, u32[]{:S(2)}) collective-permute-start(bf16[20,6,2048]{2,0,1:T(8,128)(2,1)} %get-tuple-element.229), channel_id=1, source_target_pairs={{0,1},{1,2},{2,3},{3,4},{4,5},{5,6},{6,7},{7,8},{8,9},{9,10},{10,1... | collective-permute-start | bytes 1474568 | tf_op jit(solution)/shard_map/ppermute | solution.py:23
  271.2 296.9 %collective-permute-start.3 = (bf16[20,6,2048]{2,0,1:T(8,128)(2,1)}, bf16[20,6,2048]{2,0,1:T(8,128)(2,1)}, u32[]{:S(2)}, u32[]{:S(2)}) collective-permute-start(bf16[20,6,2048]{2,0,1:T(8,128)(2,1)} %get-tuple-element.230), channel_id=1, source_target_pairs={{1,0},{2,1},{3,2},{4,3},{5,4},{6,5},{7,6},{8,7},{9,8},{10,9},{11,1... | collective-permute-start | bytes 1474568 | tf_op jit(solution)/shard_map/ppermute | solution.py:25
  568.1 2.2 copy-start.10
  568.1 2.3 copy-start.11
  568.1 2.3 copy-start.12
  570.4 2.7 copy-start.2
  575.5 2.1 copy-start.4
  577.1 1.5 copy-start.5
  577.1 1.6 copy-start.8
  584.0 3.7 copy-start.3
  587.7 2.6 copy-start.2
  592.8 2.1 copy-start.4
  594.4 1.5 copy-start.5
  594.4 1.6 copy-start.8
  601.3 3.7 copy-start.3
Sparse Core Ops, SparseCore 0:
  10.9 204.8 all-gather.1
where the time goes:
time: 614 us
  local copies, waits for them, and re-layouts  306 us (50%)
  waiting for transfers between devices  245 us (40%)
  starting transfers between devices  23 us (4%)
  matrix products  17.1 us (3%)
  between operations  13.6 us (2%)
    gather x2, local copies, waits for them, and re-layouts, per_device(): bias = rel_bias[:, idx_r, idx_c]  287 us
    all_gather x1, waiting for transfers between devices, per_device(): lax.all_gather(w_qkv, 'lon', axis=1, tiled=True)  209 us
    ppermute x2, waiting for transfers between devices, padded(): lax.ppermute(head, axis, [((i + 1) % count, i) for i in range(ends)])  32 us
  transfers between devices with their start and end apart: 5, of which 3 were waited for; matrix products, arithmetic and copies ran while one was open for 47% of the time, Pallas kernels for 0%

commit v1 on v0

--- a/solution.py
+++ b/solution.py
@@ -62,6 +62,16 @@
     )
 
 
+def bias_table(rel_bias):
+    side = TILE + 2 * RADIUS
+    reach = 2 * RADIUS + 1
+    delta = np.arange(side)[None, :] - np.arange(TILE)[:, None]
+    pick = (np.clip(delta, 0, reach - 1)[:, :, None] == np.arange(reach)).astype(np.float32)
+    rows = jnp.einsum("hrc,qkr->hqkc", rel_bias, pick, precision=lax.Precision.HIGHEST)
+    both = jnp.einsum("hqkc,xyc->hqxky", rows, pick, precision=lax.Precision.HIGHEST)
+    return both.reshape(HEADS, TILE * TILE, side * side)
+
+
 def per_device(tokens, w_qkv, rel_bias, tile_valid):
     rows, cols, width = tokens.shape
     inside, slot, onehot, idx_r, idx_c, krow = static_tables()
@@ -80,7 +90,7 @@
     keyval = qkv[:, :, width:]
     keyval = padded(keyval, (("lat", 0),), RADIUS, False)
     keyval = padded(keyval, (("lon", 1),), RADIUS, True)
-    bias = rel_bias[:, idx_r, idx_c]
+    bias = bias_table(rel_bias)
     total_rows = rows * lax.axis_size("lat")
     row_base = lax.axis_index("lat") * rows
     tiles_c = cols // TILE

time: 614 us -> 329 us (0.54)
  the two profiles are of different devices: /device:TPU:7 before, /device:TPU:1 now
where the time goes in v1:
time: 329 us; the launch traced here: 327 us
  waiting for transfers between devices  218 us (66%)
  matrix products  31.1 us (9%)
  local copies, waits for them, and re-layouts  30.4 us (9%)
  starting transfers between devices  24 us (7%)
  between operations  13.6 us (4%)
  loops' own time  5.52 us (2%)
  other arithmetic  5.03 us (2%)
    all_gather x1, waiting for transfers between devices, per_device(): lax.all_gather(w_qkv, 'lon', axis=1, tiled=True)  209 us
    dot_general x1, matrix products, bias_table(): jnp.einsum('hqkc,xyc->hqxky', rows, pick, precision=lax.Precision.HIGHEST)  13 us
    ppermute x2, starting transfers between devices, padded(): lax.ppermute(tail, axis, [(i, (i + 1) % count) for i in range(ends)])  12.8 us
    ppermute x2, starting transfers between devices, padded(): lax.ppermute(head, axis, [((i + 1) % count, i) for i in range(ends)])  11.2 us
    reshape x1, local copies, waits for them, and re-layouts, bias_table(): return both.reshape(HEADS, TILE * TILE, side * side)  8.96 us
    sub x2, matrix products, tile_attend(): expo = jnp.where(mask[None], jnp.exp(scores - top), 0.0)  7.89 us
  transfers between devices with their start and end apart: 5, of which 3 were waited for; matrix products, arithmetic and copies ran while one was open for 8% of the time, Pallas kernels for 0%

profile of v1, /device:TPU:1, one launch (start us, length us, event | category | flops | bytes accessed | tf_op | source)
XLA Modules:
  0.0 327.3 jit_solution(16051082650852943235)
XLA Ops:
  7.3 209.5 %all-gather.2.cloned.1.call-done = bf16[1024,3072]{1,0:T(8,128)(2,1)} async-done(((bf16[1024,128]{1,0:T(8,128)(2,1)}), bf16[1024,3072]{1,0:T(8,128)(2,1)}) %all-gather.2.cloned.1.call-update) | async-done | bytes 6291472 | tf_op jit(solution)/shard_map/all_gather | solution.py:83
  216.8 3.8 %convolution_convert_fusion.1 = bf16[128,3072]{1,0:T(8,128)(2,1)S(1)} fusion(bf16[128,1024]{1,0:T(8,128)(2,1)S(1)} %bitcast.59, bf16[1024,3072]{1,0:T(8,128)(2,1)} %all-gather.2.cloned.1.call-done), kind=kOutput, calls=%fused_computation.20 | convolution fusion | flops 805699584 | bytes 7340032 | tf_op jit(solution)/shard_map/dot_general | solution.py:81
  220.6 1.0 copy.34
  221.7 10.6 %collective-permute-start = (bf16[6,16,2048]{2,0,1:T(8,128)(2,1)}, bf16[6,16,2048]{2,0,1:T(8,128)(2,1)}, u32[]{:S(2)}, u32[]{:S(2)}) collective-permute-start(bf16[6,16,2048]{2,0,1:T(8,128)(2,1)} %copy.34), channel_id=1, source_target_pairs={{0,24},{24,48},{48,72},{72,96},{96,120},{120,144},{144,168},{168,1... | collective-permute-start | bytes 1179656 | tf_op jit(solution)/shard_map/ppermute | solution.py:23
  232.3 1.0 copy.36
  233.3 1.9 collective-permute-start.1
  235.3 1.0 convolution_bitcast_fusion.1
  236.7 2.0 collective-permute-done
  238.7 5.4 %collective-permute-done.1 = bf16[6,16,2048]{2,0,1:T(8,128)(2,1)} collective-permute-done((bf16[6,16,2048]{2,0,1:T(8,128)(2,1)}, bf16[6,16,2048]{2,0,1:T(8,128)(2,1)}, u32[]{:S(2)}, u32[]{:S(2)}) %collective-permute-start.1) | collective-permute-done | bytes 393248 | tf_op jit(solution)/shard_map/ppermute | solution.py:25
  244.1 2.7 pad_maximum_fusion.3
  246.8 2.2 collective-permute-start.2
  249.0 9.3 %collective-permute-start.3 = (bf16[20,6,2048]{2,0,1:T(8,128)(2,1)}, bf16[20,6,2048]{2,0,1:T(8,128)(2,1)}, u32[]{:S(2)}, u32[]{:S(2)}) collective-permute-start(bf16[20,6,2048]{2,0,1:T(8,128)(2,1)} %get-tuple-element.230), channel_id=1, source_target_pairs={{1,0},{2,1},{3,2},{4,3},{5,4},{6,5},{7,6},{8,7},{9,8},{10,9},{11,1... | collective-permute-start | bytes 1474568 | tf_op jit(solution)/shard_map/ppermute | solution.py:25
  258.3 13.0 %convolution_bitcast_fusion = f32[16,8,8,20,20]{4,3,2,1,0:T(8,128)} fusion(f32[16,8,20,13,1]{2,3,4,1,0:T(8,128)S(1)} %convolution_bitcast_fusion.1, f32[8,20,13,1,1]{1,2,0,4,3:T(8,128)S(1)} %copy-done.8), kind=kOutput, calls=%fused_computation.19 | convolution fusion | flops 63897600 | bytes 1779840 | tf_op jit(solution)/shard_map/hqkc,xyc->hqxky/dot_general | solution.py:71
  271.3 9.0 %reshape.88 = f32[16,64,400]{2,1,0:T(8,128)} reshape(f32[16,8,8,20,20]{4,3,2,1,0:T(8,128)} %convolution_bitcast_fusion) | data formatting | bytes 3276800 | tf_op jit(solution)/shard_map/reshape | solution.py:72
  280.3 0.7 slice.47
  281.0 0.8 copy-done.6
  281.8 2.2 pad_maximum_fusion
  284.1 34.7 %while.13 = (s32[]{:T(128)}, bf16[2,8,8,1024]{3,2,1,0:T(8,128)(2,1)}, s32[2]{0:T(128)S(1)}, bf16[20,28,2048]{2,0,1:T(8,128)(2,1)S(1)}, s32[1,2,9]{2,1,0:T(2,128)...) while((s32[]{:T(128)}, ...), condition=%wide.region_3.4_spmd.clone, body=%wide.region_0.3_spmd.sunk.clone.sunk | while | flops 108261176 | bytes 44236192 | solution.py:127
  284.1 0.7 dynamic_slice.51
  286.9 0.9 copy.50
  287.9 1.4 reshape.107
  289.2 1.6 fusion.38
  292.5 3.9 %fusion.41 = (f32[16,64]{1,0:T(8,128)S(1)}, f32[16,64,400]{2,1,0:T(8,128)}) fusion(pred[64,400]{1,0:T(8,128)(4,1)S(1)} %and_and_fusion.2, f32[16,64,400]{2,1,0:T(8,128)} %get-tuple-element.339, bf16[400,16,64]{0,2,1:T(8,128)(2,1)S(1)} %bitcast.60, bf16[64,16,64]{2,1,0:T(8,128)(2,1)S(1)} %reshape.108), kind=kOutput, calls=%fused_computation.29.clone.1 | convolution fusion | flops 54886800 | bytes 4256768 | tf_op jit(solution)/shard_map/while/body/eval_jaxpr/sub | solution.py:57
  296.4 1.3 copy.51
  297.7 2.6 fusion.42
  304.2 0.9 copy.50
  305.2 1.4 reshape.107
  306.6 1.6 fusion.38
  309.8 4.0 %fusion.41 = (f32[16,64]{1,0:T(8,128)S(1)}, f32[16,64,400]{2,1,0:T(8,128)}) fusion(pred[64,400]{1,0:T(8,128)(4,1)S(1)} %and_and_fusion.2, f32[16,64,400]{2,1,0:T(8,128)} %get-tuple-element.339, bf16[400,16,64]{0,2,1:T(8,128)(2,1)S(1)} %bitcast.60, bf16[64,16,64]{2,1,0:T(8,128)(2,1)S(1)} %reshape.108), kind=kOutput, calls=%fused_computation.29.clone.1 | convolution fusion | flops 54886800 | bytes 4256768 | tf_op jit(solution)/shard_map/while/body/eval_jaxpr/sub | solution.py:57
  313.7 1.3 copy.51
  315.1 2.6 fusion.42
  318.8 1.7 copy_bitcast_fusion
  (65 shorter events, 6.2 us)
Async XLA Ops:
  6.5 210.2 %copy-start = (bf16[8,16,1024]{2,1,0:T(8,128)(2,1)S(1)}, bf16[8,16,1024]{2,1,0:T(8,128)(2,1)}, u32[]{:S(2)}) copy-start(bf16[8,16,1024]{2,1,0:T(8,128)(2,1)} %param.12) | copy-start | bytes 786436
  6.5 210.2 %all-gather.2.cloned.1.call-start = ((), (), s32[]{:S(2)}) async-start(), calls=%async_computation | async-start | bytes 6553600 | tf_op jit(solution)/shard_map/all_gather | solution.py:83
  220.5 14.7 %copy-start.7 = (f32[16,13,13]{2,0,1:T(8,128)S(1)}, f32[16,13,13]{2,0,1:T(8,128)}, u32[]{:S(2)}) copy-start(f32[16,13,13]{2,0,1:T(8,128)} %param.14) | copy-start | bytes 32452
  220.5 14.7 %copy-start.9 = (f32[8,20,13,1]{1,2,0,3:T(8,128)S(1)}, f32[8,20,13,1]{1,2,0,3:T(8,128)}, u32[]{:S(2)}) copy-start(f32[8,20,13,1]{1,2,0,3:T(8,128)} %constant.131) | copy-start | bytes 24964
  221.7 17.1 %collective-permute-start = (bf16[6,16,2048]{2,0,1:T(8,128)(2,1)}, bf16[6,16,2048]{2,0,1:T(8,128)(2,1)}, u32[]{:S(2)}, u32[]{:S(2)}) collective-permute-start(bf16[6,16,2048]{2,0,1:T(8,128)(2,1)} %copy.34), channel_id=1, source_target_pairs={{0,24},{24,48},{48,72},{72,96},{96,120},{120,144},{144,168},{168,1... | collective-permute-start | bytes 1179656 | tf_op jit(solution)/shard_map/ppermute | solution.py:23
  233.3 10.8 %collective-permute-start.1 = (bf16[6,16,2048]{2,0,1:T(8,128)(2,1)}, bf16[6,16,2048]{2,0,1:T(8,128)(2,1)}, u32[]{:S(2)}, u32[]{:S(2)}) collective-permute-start(bf16[6,16,2048]{2,0,1:T(8,128)(2,1)} %copy.36), channel_id=1, source_target_pairs={{24,0},{48,24},{72,48},{96,72},{120,96},{144,120},{168,144},{192,1... | collective-permute-start | bytes 1179656 | tf_op jit(solution)/shard_map/ppermute | solution.py:25
  236.4 22.0 %copy-start.8 = (f32[8,20,13,1,1]{1,2,0,4,3:T(8,128)S(1)}, f32[8,20,13,1,1]{1,2,0,4,3:T(8,128)}, u32[]{:S(2)}) copy-start(f32[8,20,13,1,1]{1,2,0,4,3:T(8,128)} %constant.132) | copy-start | bytes 24964
  246.8 34.2 %collective-permute-start.2 = (bf16[20,6,2048]{2,0,1:T(8,128)(2,1)}, bf16[20,6,2048]{2,0,1:T(8,128)(2,1)S(1)}, u32[]{:S(2)}, u32[]{:S(2)}) collective-permute-start(bf16[20,6,2048]{2,0,1:T(8,128)(2,1)} %get-tuple-element.229), channel_id=1, source_target_pairs={{0,1},{1,2},{2,3},{3,4},{4,5},{5,6},{6,7},{7,8},{8,9},{9,10},{10,1... | collective-permute-start | bytes 1474568 | tf_op jit(solution)/shard_map/ppermute | solution.py:23
  249.0 32.8 %collective-permute-start.3 = (bf16[20,6,2048]{2,0,1:T(8,128)(2,1)}, bf16[20,6,2048]{2,0,1:T(8,128)(2,1)}, u32[]{:S(2)}, u32[]{:S(2)}) collective-permute-start(bf16[20,6,2048]{2,0,1:T(8,128)(2,1)} %get-tuple-element.230), channel_id=1, source_target_pairs={{1,0},{2,1},{3,2},{4,3},{5,4},{6,5},{7,6},{8,7},{9,8},{10,9},{11,1... | collective-permute-start | bytes 1474568 | tf_op jit(solution)/shard_map/ppermute | solution.py:25
  281.0 3.1 copy-start.10
  281.0 3.1 copy-start.11
  281.0 3.1 copy-start.12
  281.0 0.8 copy-start.6
  284.1 2.7 copy-start.1
  289.2 2.1 copy-start.3
  290.8 1.5 copy-start.4
  290.8 1.6 copy-start.5
  297.7 3.7 %copy-start.2 = (bf16[20,28,2048]{2,0,1:T(8,128)(2,1)S(1)}, bf16[20,28,2048]{2,0,1:T(8,128)(2,1)}, u32[]{:S(2)}) copy-start(bf16[20,28,2048]{2,0,1:T(8,128)(2,1)} %copy-done.1) | copy-start | bytes 6881284 | tf_op jit(solution)/shard_map/while
  301.5 2.6 copy-start.1
  306.6 2.1 copy-start.3
  308.1 1.5 copy-start.4
  308.1 1.6 copy-start.5
  315.1 3.7 %copy-start.2 = (bf16[20,28,2048]{2,0,1:T(8,128)(2,1)S(1)}, bf16[20,28,2048]{2,0,1:T(8,128)(2,1)}, u32[]{:S(2)}) copy-start(bf16[20,28,2048]{2,0,1:T(8,128)(2,1)} %copy-done.1) | copy-start | bytes 6881284 | tf_op jit(solution)/shard_map/while
Sparse Core Ops, SparseCore 0:
  10.9 205.7 all-gather.1

commit v2 on v0

v2 whole, which is shorter than its diff:
```python
import functools

import jax
import jax.numpy as jnp
from jax import lax
from jax.experimental import pallas as pl
from jax.experimental.pallas import tpu as pltpu
from jax.sharding import PartitionSpec as P

HEADS = 16
HD = 64
D = 1024
TILE = 8
RADIUS = 6
REACH = 2 * RADIUS + 1
ROWS = 256
SIDE = 28
WIDE = 32
NEG = -1e30

X = 4
Y = 8
Z = 12
COMMON = 256
PART = (D - COMMON) // 4
HALF = PART // 2


def remote(src, dst, send_sem, recv_sem, device):
    return pltpu.make_async_remote_copy(
        src_ref=src,
        dst_ref=dst,
        send_sem=send_sem,
        recv_sem=recv_sem,
        device_id=device,
        device_id_type=pl.DeviceIdType.MESH,
    )


def kernel(
    tok_ref,
    w_ref,
    line_ref,
    flag_ref,
    out_ref,
    wbuf,
    xall,
    qbuf,
    kvbuf,
    table,
    masks,
    obuf,
    sends,
    recvs,
    xsends,
    xrecvs,
    hsends,
    hrecvs,
    osends,
    orecvs,
    local,
):
    lat = lax.axis_index("lat")
    lon = lax.axis_index("lon")
    core = lat % 2
    x = (lat // 2) % X
    ylo = lat // 8
    yhi = lon // Z
    z = lon % Z
    y = yhi * 4 + ylo
    colour = (x + 2 * y) % 4

    def place(xx, yy, zz):
        return ((yy % 4) * 8 + xx * 2 + core, (yy // 4) * Z + zz)

    z_up, z_down = place(x, y, (z + 1) % Z), place(x, y, (z + Z - 1) % Z)
    x_up, x_down = place((x + 1) % X, y, z), place((x + X - 1) % X, y, z)
    y_up, y_down = place(x, (y + 1) % Y, z), place(x, (y + Y - 1) % Y, z)
    mate = (lat + 1 - 2 * core, lon)
    east, west = (lon + 1) % (2 * Z), (lon + 2 * Z - 1) % (2 * Z)
    vert = lat + 2 * core - 1
    inner = jnp.logical_and(vert >= 0, vert < ROWS // TILE)
    ends = jnp.logical_or(ylo == 0, ylo == 3)
    far_lo = jnp.where(ylo == 3, 0, 2)
    over = 4 * (1 - yhi)
    feeder = place(x, over + jnp.where(ylo < 2, 3, 0), z)

    def fed(i):
        return place(x, over + far_lo + i, z)

    middle = jnp.where(z // 4 == 1, 1, 0)
    mine = yhi == (core + middle) % 2

    def common():
        return pl.ds(0, COMMON)

    def part(c):
        return pl.ds(pl.multiple_of(COMMON + (c % 4) * PART, 16), PART)

    def first(c):
        return pl.ds(pl.multiple_of(COMMON + (c % 4) * PART, 16), HALF)

    def second(c):
        return pl.ds(pl.multiple_of(COMMON + (c % 4) * PART + HALF, 16), HALF)

    @pl.when(jnp.logical_not(inner))
    def _():
        xall[pl.ds(22 * core, RADIUS)] = jnp.zeros((RADIUS, WIDE, D), jnp.bfloat16)

    barrier = pltpu.get_barrier_semaphore()

    def hello(device):
        pl.semaphore_signal(
            barrier, inc=1, device_id=device, device_id_type=pl.DeviceIdType.MESH
        )

    for device in (
        z_up,
        z_down,
        x_up,
        x_down,
        y_up,
        y_down,
        mate,
        (lat, east),
        (lat, west),
        feeder,
    ):
        hello(device)

    @pl.when(inner)
    def _():
        for device in ((vert, lon), (vert, east), (vert, west)):
            hello(device)

    @pl.when(ends)
    def _():
        hello(fed(0))
        hello(fed(1))

    pl.semaphore_wait(barrier, 10 + jnp.where(inner, 3, 0) + jnp.where(ends, 2, 0))

    def along(p, rows, kind, landing, device):
        ref = wbuf.at[p, rows]
        return remote(ref, ref, sends.at[kind, p], recvs.at[landing, p], device)

    def pushes(p):
        return (
            along(p, part(colour), 4, 2, x_up),
            along(p, part(colour), 5, 3, x_down),
            along(p, first(colour), 6, 4, y_up),
            along(p, second(colour), 7, 5, y_down),
        )

    def behind(s):
        return (z + Z - s) % Z

    def ahead(s):
        return (z + s) % Z

    def step_sends(s, act):
        low, high = behind(s), ahead(s)

        @pl.when(s < 6)
        def _():
            act(along(low, common(), 0, 0, z_up))
            act(along(high, part(colour), 3, 1, z_down))

        @pl.when(s < 5)
        def _():
            act(along(low, part(colour), 1, 1, z_up))
            act(along(high, common(), 2, 0, z_down))

        for copy in pushes(low):
            act(copy)

        @pl.when(jnp.logical_and(s > 0, s < 6))
        def _():
            for copy in pushes(high):
                act(copy)

    def landed(p):
        along(p, common(), 0, 0, z_up).wait_recv()
        along(p, part(colour), 1, 1, z_up).wait_recv()

    def filled(p):
        along(p, part(colour + 3), 4, 2, x_up).wait_recv()
        along(p, part(colour + 1), 5, 3, x_down).wait_recv()
        along(p, first(colour + 2), 6, 4, y_up).wait_recv()
        along(p, second(colour + 2), 7, 5, y_down).wait_recv()

    def start(copy):
        copy.start()

    def ring_step(s):
        landed(behind(s))

        @pl.when(s < 6)
        def _():
            landed(ahead(s))

        step_sends(s, start)

    def own_copies():
        return (
            pltpu.make_async_copy(w_ref.at[common()], wbuf.at[z, common()], local.at[0]),
            pltpu.make_async_copy(w_ref.at[part(colour)], wbuf.at[z, part(colour)], local.at[1]),
        )

    def feed_copies():
        copies = []
        for i in range(2):
            tint = x + 2 * (over + far_lo + i)
            for k, rows in enumerate((common(), part(tint))):
                copies.append(
                    remote(
                        w_ref.at[rows],
                        wbuf.at[z, rows],
                        xsends.at[2 * i + k],
                        xrecvs.at[k],
                        fed(i),
                    )
                )
        return copies

    @pl.when(jnp.logical_and(mine, ends))
    def _():
        for copy in feed_copies():
            copy.start()

    @pl.when(mine)
    def _():
        for copy in own_copies():
            copy.start()
        for copy in own_copies():
            copy.wait()

    mid = 6 + 8 * core
    edge = 22 * core
    theirs = 22 - 22 * core
    give = 2 * core

    def halo_copies():
        return (
            remote(
                tok_ref.at[:, 8:16],
                xall.at[pl.ds(mid, 8), 0:8],
                hsends.at[0],
                hrecvs.at[0],
                (lat, east),
            ),
            remote(
                tok_ref.at[:, 0:8],
                xall.at[pl.ds(mid, 8), 24:32],
                hsends.at[1],
                hrecvs.at[1],
                (lat, west),
            ),
        )

    def pole_copies():
        give_rows = pl.ds(give, RADIUS)

        def one(dst_row):
            land = pl.ds(dst_row, RADIUS)
            return (
                remote(
                    tok_ref.at[give_rows],
                    xall.at[land, 8:24],
                    hsends.at[2],
                    hrecvs.at[2],
                    (vert, lon),
                ),
                remote(
                    tok_ref.at[give_rows, 8:16],
                    xall.at[land, 0:8],
                    hsends.at[3],
                    hrecvs.at[3],
                    (vert, east),
                ),
                remote(
                    tok_ref.at[give_rows, 0:8],
                    xall.at[land, 24:32],
                    hsends.at[4],
                    hrecvs.at[4],
                    (vert, west),
                ),
            )

        return one

    def mate_copy(half):
        rows = pl.ds(14 * half, 14)
        return remote(xall.at[rows], xall.at[rows], hsends.at[5], hrecvs.at[5], mate)

    def mask_copy(half):
        return remote(masks.at[half], masks.at[half], hsends.at[6], hrecvs.at[6], mate)

    own_tokens = pltpu.make_async_copy(tok_ref, xall.at[pl.ds(mid, 8), 8:24], local.at[2])
    own_tokens.start()
    for copy in halo_copies():
        copy.start()

    @pl.when(inner)
    def _():
        for copy in pole_copies()(theirs):
            copy.start()

    @pl.when(jnp.logical_not(mine))
    def _():
        for k, rows in enumerate((common(), part(colour))):
            remote(
                w_ref.at[rows], wbuf.at[z, rows], xsends.at[k], xrecvs.at[k], feeder
            ).wait_recv()

    step_sends(0, start)

    lane = lax.broadcasted_iota(jnp.int32, (TILE, 20 * WIDE), 1)
    krow = lane // WIDE
    kcol = lane % WIDE
    up = (krow + 2) // TILE
    grow = lat * TILE + krow - RADIUS
    exists = jnp.logical_and(grow >= 0, grow < ROWS)
    for tc in range(2):
        side = kcol // TILE - tc
        level = jnp.full(lane.shape, NEG, jnp.float32)
        for du in range(3):
            for dv in range(3):
                slot = 3 * du + dv
                value = 0.0
                if slot != 4:
                    value = jnp.where(flag_ref[0, tc, slot] > 0, 0.0, NEG)
                level = jnp.where(jnp.logical_and(up == du, side == dv), value, level)
        masks[core, tc] = jnp.where(exists, level, NEG)
    mask_copy(core).start()

    ring_step(1)

    for h in range(HEADS // 2):
        line = line_ref[pl.ds(8 * core + h, 1), :]
        spread = jnp.broadcast_to(line, (16, 512))
        for qr in range(4):
            start_row = 64 * (h % 2) + 16 * qr
            table[h // 2, start_row : start_row + 16, :] = pltpu.roll(
                spread, WIDE * qr + 2, 1, stride=1, stride_axis=0
            )

    for copy in halo_copies():
        copy.wait_recv()

    @pl.when(inner)
    def _():
        for copy in pole_copies()(edge):
            copy.wait_recv()

    own_tokens.wait()
    mate_copy(core).start()

    ring_step(2)
    mate_copy(1 - core).wait_recv()
    mask_copy(1 - core).wait_recv()
    ring_step(3)

    lane = lax.broadcasted_iota(jnp.int32, (256, 128), 1)

    def project(p):
        j = p % 4
        role = (3 + core - p // 4) % 3

        @pl.when(role == 0)
        def _():
            q = jnp.dot(
                xall[6:22, 8:24, :].reshape(256, D), wbuf[p], preferred_element_type=jnp.float32
            )
            q = q * (1.0 / HD**0.5)
            qbuf[j, 0] = jnp.where(lane < HD, q, 0.0).astype(jnp.bfloat16)
            qbuf[j, 1] = jnp.where(lane < HD, 0.0, q).astype(jnp.bfloat16)

        @pl.when(role > 0)
        def _():
            kvbuf[role - 1, j] = jnp.dot(
                xall[...].reshape(SIDE * WIDE, D), wbuf[p], preferred_element_type=jnp.float32
            ).astype(jnp.bfloat16)

    def consume(i, carry):
        d = (i + 1) // 2
        odd = i % 2

        @pl.when(jnp.logical_and(odd == 1, jnp.logical_and(d >= 3, d < 6)))
        def _():
            ring_step(d + 1)

        p = (z + Z + jnp.where(odd == 1, -d, d)) % Z
        filled(p)
        project(p)
        return carry

    lax.fori_loop(0, Z, consume, 0)

    small = lax.broadcasted_iota(jnp.int32, (64, 128), 1)

    def attend(j, band):
        q = qbuf[j, :, pl.ds(pl.multiple_of(64 * band, 64), 64), :].reshape(128, 128)
        keys = pl.ds(pl.multiple_of(128 * band, 128), 512)
        k = kvbuf[0, j, keys, :]
        v = kvbuf[1, j, keys, :]
        score = lax.dot_general(
            q, k, (((1,), (1,)), ((), ())), preferred_element_type=jnp.float32
        )
        shift = pl.multiple_of(128 * (band % 2), 128)
        mask = masks[band // 2, :, :, pl.ds(shift, 512)]
        score = (score + table[j]).reshape(8, 2, TILE, 512) + mask[None]
        score = score.reshape(128, 512)
        top = jnp.max(score, axis=1, keepdims=True)
        expo = jnp.exp(score - top)
        total = jnp.sum(expo, axis=1, keepdims=True)
        weight = (expo * (1.0 / total)).astype(jnp.bfloat16)
        both = jnp.dot(weight, v, preferred_element_type=jnp.float32)
        return jnp.where(small < HD, both[:64], both[64:]).astype(jnp.bfloat16)

    def block(j):
        return pl.ds(pl.multiple_of(128 * (4 * core + j), 128), 128)

    def out_copy(j, cols):
        return remote(obuf.at[j], out_ref.at[:, cols], osends.at[j], orecvs.at[j], mate)

    def heads(j, carry):
        for i in range(2):
            obuf[j, 64 * i : 64 * i + 64, :] = attend(j, 2 * (1 - core) + i)
        out_copy(j, block(j)).start()
        for i in range(2):
            out_ref[64 * i : 64 * i + 64, block(j)] = attend(j, 2 * core + i)
        return carry

    lax.fori_loop(0, 4, heads, 0)

    def done(copy):
        copy.wait_send()

    def drain(s, carry):
        step_sends(s, done)
        return carry

    lax.fori_loop(0, 7, drain, 0)

    @pl.when(jnp.logical_and(mine, ends))
    def _():
        for copy in feed_copies():
            copy.wait_send()

    for copy in halo_copies():
        copy.wait_send()

    @pl.when(inner)
    def _():
        for copy in pole_copies()(theirs):
            copy.wait_send()

    mate_copy(core).wait_send()
    mask_copy(core).wait_send()
    for j in range(4):
        cols = pl.ds(pl.multiple_of(128 * (4 * (1 - core) + j), 128), 128)
        out_copy(j, block(j)).wait_send()
        out_copy(j, cols).wait_recv()


def per_device(tokens, w_qkv, rel_bias, tile_valid):
    rows, cols, width = tokens.shape
    line = jnp.pad(
        rel_bias,
        ((0, 0), (0, 16 - REACH), (0, WIDE - REACH)),
        constant_values=NEG,
    ).reshape(HEADS, 16 * WIDE)
    vmem = pl.BlockSpec(memory_space=pltpu.VMEM)
    dma = pltpu.SemaphoreType.DMA
    out = pl.pallas_call(
        kernel,
        out_shape=jax.ShapeDtypeStruct((rows * cols, width), jnp.bfloat16),
        in_specs=[vmem, vmem, vmem, pl.BlockSpec(memory_space=pltpu.SMEM)],
        out_specs=vmem,
        scratch_shapes=[
            pltpu.VMEM((Z, D, 128), jnp.bfloat16),
            pltpu.VMEM((SIDE, WIDE, D), jnp.bfloat16),
            pltpu.VMEM((4, 2, 256, 128), jnp.bfloat16),
            pltpu.VMEM((2, 4, SIDE * WIDE, 128), jnp.bfloat16),
            pltpu.VMEM((4, 128, 512), jnp.float32),
            pltpu.VMEM((2, 2, TILE, 20 * WIDE), jnp.float32),
            pltpu.VMEM((4, 128, 128), jnp.bfloat16),
            dma((8, Z)),
            dma((6, Z)),
            dma((4,)),
            dma((2,)),
            dma((7,)),
            dma((7,)),
            dma((4,)),
            dma((4,)),
            dma((3,)),
        ],
        compiler_params=pltpu.CompilerParams(
            collective_id=0, has_side_effects=True, vmem_limit_bytes=48 << 20
        ),
    )(tokens, w_qkv, line, tile_valid)
    return out.reshape(rows, cols, width)


def solution(mesh):
    placed = (P("lat", "lon", None), P(None, "lon"), P(), P("lat", "lon", None))
    return jax.shard_map(
        per_device, mesh=mesh, in_specs=placed, out_specs=P("lat", "lon", None), check_vma=False
    )
```

time: 614 us -> 79.2 us (0.13)
  the two profiles are of different devices: /device:TPU:7 before, /device:TPU:1 now
where the time goes in v2:
time: 79.2 us; the launch traced here: 77.9 us
  Pallas kernels  75.3 us (95%)
  local copies, waits for them, and re-layouts  2.61 us (3%)
    pallas_call x1, Pallas kernels, per_device(): pl.pallas_call(kernel, out_shape=jax.ShapeDtypeStruct((rows * cols, width...  75.3 us
    unnamed x8, local copies, waits for them, and re-layouts  2.5 us

profile of v2, /device:TPU:1, one launch (start us, length us, event | category | flops | bytes accessed | tf_op | source)
XLA Modules:
  0.0 77.9 jit_solution(6917827803388485795)
XLA Ops:
  0.0 0.0 copy-start.1
  0.0 1.0 %copy.6 = f32[16,13,13]{2,1,0:T(8,128)S(1)} copy(f32[16,13,13]{2,0,1:T(8,128)} %param.6) | data formatting | bytes 21632
  1.0 0.0 copy-start
  1.0 0.0 copy-start.2
  1.0 0.1 reshape.6.line_ref
  1.1 0.0 copy-done.1
  1.1 0.8 %copy-done = bf16[8,16,1024]{2,1,0:T(8,128)(2,1)S(1)} copy-done((bf16[8,16,1024]{2,1,0:T(8,128)(2,1)S(1)}, bf16[8,16,1024]{2,1,0:T(8,128)(2,1)}, u32[]{:S(2)}) %copy-start) | copy-done | bytes 262168
  1.9 0.0 copy-done.2
  1.9 75.3 %shard_map.46 = bf16[128,1024]{1,0:T(8,128)(2,1)S(1)} custom-call(bf16[8,16,1024]{2,1,0:T(8,128)(2,1)S(1)} %copy-done, bf16[1024,128]{1,0:T(8,128)(2,1)S(1)} %copy-done.1, f32[16,512]{1,0:T(8,128)S(1)} %reshape.6.line_ref, s32[1,2,9]{2,1,0:T(2,128)S(1)} %copy-done.2), custom_call_target="tpu_custom_call" | custom-call | tf_op jit(solution)/shard_map/pallas_call | solution.py:476
  77.2 0.7 copy.8
  (1 shorter events, 0.0 us)
Async XLA Ops:
  0.0 1.1 %copy-start.1 = (bf16[1024,128]{1,0:T(8,128)(2,1)S(1)}, bf16[1024,128]{1,0:T(8,128)(2,1)}, u32[]{:S(2)}) copy-start(bf16[1024,128]{1,0:T(8,128)(2,1)} %w_ref.1) | copy-start | bytes 786436
  1.0 1.0 %copy-start = (bf16[8,16,1024]{2,1,0:T(8,128)(2,1)S(1)}, bf16[8,16,1024]{2,1,0:T(8,128)(2,1)}, u32[]{:S(2)}) copy-start(bf16[8,16,1024]{2,1,0:T(8,128)(2,1)} %tok_ref.1) | copy-start | bytes 786436
  1.0 0.9 %copy-start.2 = (s32[1,2,9]{2,1,0:T(2,128)S(1)}, s32[1,2,9]{2,1,0:T(2,128)}, u32[]{:S(2)}) copy-start(s32[1,2,9]{2,1,0:T(2,128)} %flag_ref.1) | copy-start | bytes 220

commit v3 on v2

v3 whole, which is shorter than its diff:
```python
import functools

import jax
import jax.numpy as jnp
from jax import lax
from jax.experimental import pallas as pl
from jax.experimental.pallas import tpu as pltpu
from jax.sharding import PartitionSpec as P

HEADS = 16
HD = 64
D = 1024
TILE = 8
RADIUS = 6
REACH = 2 * RADIUS + 1
ROWS = 256
SIDE = 28
WIDE = 32
NEG = -1e30

X = 4
Y = 8
Z = 12
STRIDE = 2
PART = D // 4
HALF = PART // 2


def remote(src, dst, send_sem, recv_sem, device):
    return pltpu.make_async_remote_copy(
        src_ref=src,
        dst_ref=dst,
        send_sem=send_sem,
        recv_sem=recv_sem,
        device_id=device,
        device_id_type=pl.DeviceIdType.MESH,
    )


def kernel(
    tok_ref,
    w_ref,
    bias_ref,
    flag_ref,
    out_ref,
    wbuf,
    xall,
    qbuf,
    kvbuf,
    lines,
    table,
    masks,
    obuf,
    sends,
    recvs,
    xsends,
    xrecvs,
    hsends,
    hrecvs,
    osends,
    orecvs,
    local,
    token,
    opened,
    reached,
):
    lat = lax.axis_index("lat")
    lon = lax.axis_index("lon")
    core = lat % 2
    x = (lat // 2) % X
    ylo = lat // 8
    yhi = lon // Z
    z = lon % Z
    y = yhi * 4 + ylo
    colour = (x + 2 * y) % 4

    def place(xx, yy, zz):
        return ((yy % 4) * 8 + xx * 2 + core, (yy // 4) * Z + zz)

    ups = [place(x, y, (z + i) % Z) for i in range(1, STRIDE + 1)]
    downs = [place(x, y, (z + Z - i) % Z) for i in range(1, STRIDE + 1)]
    x_up, x_down = place((x + 1) % X, y, z), place((x + X - 1) % X, y, z)
    y_up, y_down = place(x, (y + 1) % Y, z), place(x, (y + Y - 1) % Y, z)
    mate = (lat + 1 - 2 * core, lon)
    east, west = (lon + 1) % (2 * Z), (lon + 2 * Z - 1) % (2 * Z)
    vert = lat + 2 * core - 1
    inner = jnp.logical_and(vert >= 0, vert < ROWS // TILE)
    ends = jnp.logical_or(ylo == 0, ylo == 3)
    far_lo = jnp.where(ylo == 3, 0, 2)
    over = 4 * (1 - yhi)
    feeder = place(x, over + jnp.where(ylo < 2, 3, 0), z)

    def fed(i):
        return place(x, over + far_lo + i, z)

    middle = jnp.where(z // 4 == 1, 1, 0)
    mine = yhi == (core + middle) % 2

    def part(c):
        return pl.ds(pl.multiple_of((c % 4) * PART, PART), PART)

    def first(c):
        return pl.ds(pl.multiple_of((c % 4) * PART, PART), HALF)

    def second(c):
        return pl.ds(pl.multiple_of((c % 4) * PART + HALF, HALF), HALF)

    mid = 6 + 8 * core
    own_tokens = pltpu.make_async_copy(tok_ref, xall.at[pl.ds(mid, 8), 8:24], local.at[1])
    own_tokens.start()
    own_weights = pltpu.make_async_copy(
        w_ref.at[part(colour)], wbuf.at[z, part(colour)], local.at[0]
    )

    @pl.when(mine)
    def _():
        own_weights.start()

    @pl.when(jnp.logical_not(inner))
    def _():
        xall[pl.ds(22 * core, RADIUS)] = jnp.zeros((RADIUS, WIDE, D), jnp.bfloat16)

    barrier = pltpu.get_barrier_semaphore()

    def hello(device):
        pl.semaphore_signal(
            barrier, inc=1, device_id=device, device_id_type=pl.DeviceIdType.MESH
        )

    for device in (x_up, x_down, y_up, y_down, mate, feeder):
        hello(device)
    count = 6
    opposite = (lon + Z) % (2 * Z)
    for some, devices in (
        (ends, (fed(0), fed(1))),
        (inner, ((vert, lon),)),
        (z <= Z - 2, (ups[0],)),
        (z <= Z - 3, (ups[1],)),
        (z >= 1, (downs[0],)),
        (z >= 2, (downs[1],)),
        (jnp.logical_and(inner, z < Z - 1), ((vert, east),)),
        (jnp.logical_and(inner, z > 0), ((vert, west),)),
        (z == 0, ((lat, opposite),)),
        (jnp.logical_and(inner, z == 0), ((vert, opposite),)),
    ):
        count = count + jnp.where(some, len(devices), 0)

        @pl.when(some)
        def _():
            for device in devices:
                hello(device)

    pl.semaphore_wait(barrier, count)

    @pl.when(z > 0)
    def _():
        pl.semaphore_wait(token, 1)

    @pl.when(z < Z - 1)
    def _():
        pl.semaphore_signal(
            token, inc=1, device_id=ups[0], device_id_type=pl.DeviceIdType.MESH
        )

    def tell(semaphore, device):
        pl.semaphore_signal(
            semaphore, inc=1, device_id=device, device_id_type=pl.DeviceIdType.MESH
        )

    @pl.when(z == Z - 1)
    def _():
        tell(opened, ups[0])
        tell(opened, ups[1])
        tell(reached, (lat, east))

        @pl.when(inner)
        def _():
            tell(reached, (vert, east))

    @pl.when(z == Z - 2)
    def _():
        tell(opened, ups[1])

    def along(p, rows, kind, landing, device):
        ref = wbuf.at[p, rows]
        return remote(ref, ref, sends.at[kind, p], recvs.at[landing, p], device)

    def behind(d):
        return (z + Z - d) % Z

    def ahead(d):
        return (z + d) % Z

    def relay_up(d, act):
        p = behind(d)

        @pl.when(jnp.logical_and(d % STRIDE == 0, d < 6))
        def _():
            act(along(p, part(colour), 0, 0, ups[0]))

            @pl.when(d < 4)
            def _():
                act(along(p, part(colour), 1, 0, ups[1]))

            @pl.when(jnp.logical_and(d == 4, p < 6))
            def _():
                act(along(p, part(colour), 1, 0, ups[1]))

    def relay_down(d, act, crossing):
        p = ahead(d)
        for i in range(STRIDE):
            here = (z < i + 1) if crossing else (z >= i + 1)

            @pl.when(jnp.logical_and(here, jnp.logical_and(d % STRIDE == 0, d < 6)))
            def _():
                if i == 0:
                    act(along(p, part(colour), 2, 0, downs[0]))
                else:

                    @pl.when(d < 4)
                    def _():
                        act(along(p, part(colour), 3, 0, downs[1]))

                    @pl.when(jnp.logical_and(d == 4, p >= 6))
                    def _():
                        act(along(p, part(colour), 3, 0, downs[1]))

    def pushes(p):
        kind = 2 * STRIDE
        return [
            along(p, part(colour), kind, 2, x_up),
            along(p, part(colour), kind + 1, 3, x_down),
            along(p, first(colour), kind + 2, 4, y_up),
            along(p, second(colour), kind + 3, 5, y_down),
        ]

    def start(copy):
        copy.start()

    def finish(copy):
        copy.wait_send()

    def own_out():
        relay_up(0, start)
        relay_down(0, start, False)
        for copy in pushes(z):
            copy.start()

    def whole_in(p):
        along(p, part(colour), 0, 0, ups[0]).wait_recv()

    def pass_on(i, late):
        d = jnp.where(i < 4, i + 2 - 2 * (i % 2), i + 1)

        @pl.when(jnp.logical_and(d < 6, (d > z) == late))
        def _():
            whole_in(behind(d))
            relay_up(d, start)
            for copy in pushes(behind(d)):
                copy.start()

        @pl.when(jnp.logical_and(d < 6, (z + d >= Z) == late))
        def _():
            whole_in(ahead(d))
            relay_down(d, start, False)
            for copy in pushes(ahead(d)):
                copy.start()

        if late:

            @pl.when(d == 6)
            def _():
                whole_in(behind(d))
                for copy in pushes(behind(d)):
                    copy.start()

    def early_shards():
        def body(i, carry):
            pass_on(i, False)
            return carry

        lax.fori_loop(0, 5, body, 0)

    def late_shards(low, high):
        def body(i, carry):
            pass_on(i, True)
            return carry

        lax.fori_loop(low, high, body, 0)

    def cross_down():
        def body(i, carry):
            relay_down(2 * i, start, True)
            return carry

        lax.fori_loop(0, 3, body, 0)

    def drain():
        def body(d, carry):
            relay_up(d, finish)
            relay_down(d, finish, False)
            relay_down(d, finish, True)
            for copy in pushes(behind(d)):
                copy.wait_send()

            @pl.when(jnp.logical_and(d > 0, d < 6))
            def _():
                for copy in pushes(ahead(d)):
                    copy.wait_send()

            return carry

        lax.fori_loop(0, 7, body, 0)

    def filled(p):
        along(p, part(colour + 3), 0, 2, x_up).wait_recv()
        along(p, part(colour + 1), 0, 3, x_down).wait_recv()
        along(p, first(colour + 2), 0, 4, y_up).wait_recv()
        along(p, second(colour + 2), 0, 5, y_down).wait_recv()

    def feed(i):
        rows = part(x + 2 * (over + far_lo + i))
        return remote(w_ref.at[rows], wbuf.at[z, rows], xsends.at[i], xrecvs.at[0], fed(i))

    @pl.when(jnp.logical_and(mine, ends))
    def _():
        feed(0).start()
        feed(1).start()

    @pl.when(mine)
    def _():
        own_weights.wait()
        own_out()

    edge = 22 * core
    theirs = 22 - 22 * core
    give = 2 * core

    def halo_copies(*which):
        pairs = ((tok_ref.at[:, 8:16], 0, east), (tok_ref.at[:, 0:8], 24, west))
        copies = []
        for k in which:
            src, col, to = pairs[k]
            dst = xall.at[pl.ds(mid, 8), col : col + 8]
            copies.append(remote(src, dst, hsends.at[k], hrecvs.at[k], (lat, to)))
        return copies

    def pole_copies(*which):
        give_rows = pl.ds(give, RADIUS)

        def one(dst_row):
            land = pl.ds(dst_row, RADIUS)
            cuts = ((0, 16, 8, lon), (8, 16, 0, east), (0, 8, 24, west))
            copies = []
            for k in which:
                a, b, col, to = cuts[k]
                src = tok_ref.at[give_rows, a:b]
                dst = xall.at[land, col : col + b - a]
                copies.append(remote(src, dst, hsends.at[2 + k], hrecvs.at[2 + k], (vert, to)))
            return copies

        return one

    def mate_copy(half):
        rows = pl.ds(14 * half, 14)
        return remote(xall.at[rows], xall.at[rows], hsends.at[5], hrecvs.at[5], mate)

    def mask_copy(half):
        return remote(masks.at[half], masks.at[half], hsends.at[6], hrecvs.at[6], mate)

    def halo_west():
        halo_copies(1)[0].start()

        @pl.when(inner)
        def _():
            pole_copies(2)(theirs)[0].start()

    halo_copies(0)[0].start()

    @pl.when(inner)
    def _():
        for copy in pole_copies(0, 1)(theirs):
            copy.start()

    @pl.when(z > 0)
    def _():
        halo_west()

    @pl.when(jnp.logical_not(mine))
    def _():
        rows = part(colour)
        remote(w_ref.at[rows], wbuf.at[z, rows], xsends.at[0], xrecvs.at[0], feeder).wait_recv()
        own_out()

    lane = lax.broadcasted_iota(jnp.int32, (TILE, 20 * WIDE), 1)
    krow = lane // WIDE
    kcol = lane % WIDE
    up = (krow + 2) // TILE
    grow = lat * TILE + krow - RADIUS
    exists = jnp.logical_and(grow >= 0, grow < ROWS)
    for tc in range(2):
        side = kcol // TILE - tc
        level = jnp.full(lane.shape, NEG, jnp.float32)
        for du in range(3):
            for dv in range(3):
                slot = 3 * du + dv
                value = 0.0
                if slot != 4:
                    value = jnp.where(flag_ref[0, tc, slot] > 0, 0.0, NEG)
                level = jnp.where(jnp.logical_and(up == du, side == dv), value, level)
        masks[core, tc] = jnp.where(exists, level, NEG)
    mask_copy(core).start()

    lines[...] = jnp.full(lines.shape, NEG, jnp.float32)
    for a in range(REACH):
        lines[:, WIDE * a : WIDE * a + REACH] = bias_ref[a]
    for h in range(HEADS // 2):
        line = lines[pl.ds(8 * core + h, 1), :]
        spread = jnp.broadcast_to(line, (16, 512))
        for qr in range(4):
            start_row = 64 * (h % 2) + 16 * qr
            table[h // 2, start_row : start_row + 16, :] = pltpu.roll(
                spread, WIDE * qr + 2, 1, stride=1, stride_axis=0
            )

    lane = lax.broadcasted_iota(jnp.int32, (256, 128), 1)

    def project(p):
        j = p % 4
        role = (3 + core - p // 4) % 3

        @pl.when(role == 0)
        def _():
            q = jnp.dot(
                xall[6:22, 8:24, :].reshape(256, D), wbuf[p], preferred_element_type=jnp.float32
            )
            q = q * (1.0 / HD**0.5)
            qbuf[j, 0] = jnp.where(lane < HD, q, 0.0).astype(jnp.bfloat16)
            qbuf[j, 1] = jnp.where(lane < HD, 0.0, q).astype(jnp.bfloat16)

        @pl.when(role > 0)
        def _():
            kvbuf[role - 1, j] = jnp.dot(
                xall[...].reshape(SIDE * WIDE, D), wbuf[p], preferred_element_type=jnp.float32
            ).astype(jnp.bfloat16)

    def consume(i, late):
        d = (i + 1) // 2
        p = jnp.where(i % 2 == 1, behind(d), ahead(d))
        far = jnp.where(i % 2 == 1, d > z, z + d >= Z)

        @pl.when(jnp.logical_or(far, d == 6) == late)
        def _():
            filled(p)
            project(p)

    small = lax.broadcasted_iota(jnp.int32, (64, 128), 1)

    def attend(j, band):
        q = qbuf[j, :, pl.ds(pl.multiple_of(64 * band, 64), 64), :].reshape(128, 128)
        keys = pl.ds(pl.multiple_of(128 * band, 128), 512)
        k = kvbuf[0, j, keys, :]
        v = kvbuf[1, j, keys, :]
        score = lax.dot_general(
            q, k, (((1,), (1,)), ((), ())), preferred_element_type=jnp.float32
        )
        shift = pl.multiple_of(128 * (band % 2), 128)
        mask = masks[band // 2, :, :, pl.ds(shift, 512)]
        score = (score + table[j]).reshape(8, 2, TILE, 512) + mask[None]
        score = score.reshape(128, 512)
        top = jnp.max(score, axis=1, keepdims=True)
        expo = jnp.exp(score - top)
        total = jnp.sum(expo, axis=1, keepdims=True)
        both = jnp.dot(expo.astype(jnp.bfloat16), v, preferred_element_type=jnp.float32)
        both = both * (1.0 / total)
        return jnp.where(small < HD, both[:64], both[64:]).astype(jnp.bfloat16)

    def block(j):
        return pl.ds(pl.multiple_of(128 * (4 * core + j), 128), 128)

    def out_copy(j, cols):
        return remote(obuf.at[j], out_ref.at[:, cols], osends.at[j], orecvs.at[j], mate)

    def heads(i, carry):
        j = (z + jnp.where(i < 2, i, 5 - i)) % 4
        for b in range(2):
            obuf[j, 64 * b : 64 * b + 64, :] = attend(j, 2 * (1 - core) + b)
        out_copy(j, block(j)).start()
        for b in range(2):
            out_ref[64 * b : 64 * b + 64, block(j)] = attend(j, 2 * core + b)
        return carry

    def tokens_in():
        for copy in halo_copies(0, 1):
            copy.wait_recv()

        @pl.when(inner)
        def _():
            for copy in pole_copies(0, 1, 2)(edge):
                copy.wait_recv()

        own_tokens.wait()
        mate_copy(core).start()

    def region_in():
        mate_copy(1 - core).wait_recv()
        mask_copy(1 - core).wait_recv()

    def open_wrap():
        @pl.when(z < STRIDE)
        def _():
            pl.semaphore_wait(opened, STRIDE - z)

            @pl.when(z == 0)
            def _():
                pl.semaphore_wait(reached, 1 + jnp.where(inner, 1, 0))
                halo_west()

            cross_down()

    def project_shards(low, high, late):
        def body(i, carry):
            consume(i, late)
            return carry

        lax.fori_loop(low, high, body, 0)

    def attend_pairs(low, high):
        lax.fori_loop(low, high, heads, 0)

    early_shards()
    open_wrap()
    late_shards(0, 2)
    tokens_in()
    late_shards(2, 4)
    region_in()
    project_shards(0, 5, False)
    late_shards(4, 6)
    project_shards(5, 11, False)
    project_shards(1, 12, True)
    attend_pairs(0, 4)

    drain()

    @pl.when(jnp.logical_and(mine, ends))
    def _():
        feed(0).wait_send()
        feed(1).wait_send()

    for copy in halo_copies(0, 1):
        copy.wait_send()

    @pl.when(inner)
    def _():
        for copy in pole_copies(0, 1, 2)(theirs):
            copy.wait_send()

    mate_copy(core).wait_send()
    mask_copy(core).wait_send()
    for j in range(4):
        cols = pl.ds(pl.multiple_of(128 * (4 * (1 - core) + j), 128), 128)
        out_copy(j, block(j)).wait_send()
        out_copy(j, cols).wait_recv()


def per_device(tokens, w_qkv, rel_bias, tile_valid):
    rows, cols, width = tokens.shape
    vmem = pl.BlockSpec(memory_space=pltpu.VMEM)
    hbm = pl.BlockSpec(memory_space=pl.ANY)
    dma = pltpu.SemaphoreType.DMA
    out = pl.pallas_call(
        kernel,
        out_shape=jax.ShapeDtypeStruct((rows * cols, width), jnp.bfloat16),
        in_specs=[hbm, hbm, vmem, pl.BlockSpec(memory_space=pltpu.SMEM)],
        out_specs=vmem,
        scratch_shapes=[
            pltpu.VMEM((Z, D, 128), jnp.bfloat16),
            pltpu.VMEM((SIDE, WIDE, D), jnp.bfloat16),
            pltpu.VMEM((4, 2, 256, 128), jnp.bfloat16),
            pltpu.VMEM((2, 4, SIDE * WIDE, 128), jnp.bfloat16),
            pltpu.VMEM((HEADS, 512), jnp.float32),
            pltpu.VMEM((4, 128, 512), jnp.float32),
            pltpu.VMEM((2, 2, TILE, 20 * WIDE), jnp.float32),
            pltpu.VMEM((4, 128, 128), jnp.bfloat16),
            dma((2 * STRIDE + 4, Z)),
            dma((6, Z)),
            dma((2,)),
            dma((1,)),
            dma((7,)),
            dma((7,)),
            dma((4,)),
            dma((4,)),
            dma((2,)),
            pltpu.SemaphoreType.REGULAR,
            pltpu.SemaphoreType.REGULAR,
            pltpu.SemaphoreType.REGULAR,
        ],
        compiler_params=pltpu.CompilerParams(
            collective_id=0, has_side_effects=True, vmem_limit_bytes=63 << 20
        ),
    )(tokens, w_qkv, jnp.transpose(rel_bias, (1, 0, 2)), tile_valid)
    return out.reshape(rows, cols, width)


def solution(mesh):
    placed = (P("lat", "lon", None), P(None, "lon"), P(), P("lat", "lon", None))
    return jax.shard_map(
        per_device, mesh=mesh, in_specs=placed, out_specs=P("lat", "lon", None), check_vma=False
    )
```

time: 79.2 us -> 60.1 us (0.76)
  the two profiles are of different devices: /device:TPU:1 before, /device:TPU:497 now
where the time goes in v3:
time: 60.1 us; the launch traced here: 59.9 us
  Pallas kernels  58.2 us (97%)
  local copies, waits for them, and re-layouts  1.67 us (3%)
    pallas_call x1, Pallas kernels, per_device(): pl.pallas_call(kernel, out_shape=jax.ShapeDtypeStruct((rows * cols, width...  58.2 us
    unnamed x1, local copies, waits for them, and re-layouts  1.67 us

profile of v3, /device:TPU:497, one launch (start us, length us, event | category | flops | bytes accessed | tf_op | source)
XLA Modules:
  0.0 59.9 jit_solution(17636102696877194886)
XLA Ops:
  0.0 58.2 %shard_map.46 = bf16[128,1024]{1,0:T(8,128)(2,1)} custom-call(bf16[8,16,1024]{2,1,0:T(8,128)(2,1)} %tok_ref.1, bf16[1024,128]{1,0:T(8,128)(2,1)} %w_ref.1, f32[13,16,13]{2,1,0:T(8,128)} %bitcast.3, s32[1,2,9]{2,1,0:T(2,128)} %flag_ref.1), custom_call_target="tpu_custom_call" | custom-call | tf_op jit(solution)/shard_map/pallas_call | solution.py:571
  58.2 1.7 %copy.6 = bf16[8,16,1024]{2,1,0:T(8,128)(2,1)} copy(bf16[8,16,1024]{2,1,0:T(8,128)(2,1)} %bitcast.2) | data formatting | bytes 524288

commit v4 on v3

--- a/solution.py
+++ b/solution.py
@@ -105,21 +105,6 @@
     def second(c):
         return pl.ds(pl.multiple_of((c % 4) * PART + HALF, HALF), HALF)
 
-    mid = 6 + 8 * core
-    own_tokens = pltpu.make_async_copy(tok_ref, xall.at[pl.ds(mid, 8), 8:24], local.at[1])
-    own_tokens.start()
-    own_weights = pltpu.make_async_copy(
-        w_ref.at[part(colour)], wbuf.at[z, part(colour)], local.at[0]
-    )
-
-    @pl.when(mine)
-    def _():
-        own_weights.start()
-
-    @pl.when(jnp.logical_not(inner))
-    def _():
-        xall[pl.ds(22 * core, RADIUS)] = jnp.zeros((RADIUS, WIDE, D), jnp.bfloat16)
-
     barrier = pltpu.get_barrier_semaphore()
 
     def hello(device):
@@ -150,23 +135,51 @@
             for device in devices:
                 hello(device)
 
+    mid = 6 + 8 * core
+    own_tokens = pltpu.make_async_copy(tok_ref, xall.at[pl.ds(mid, 8), 8:24], local.at[1])
+    own_tokens.start()
+    own_weights = pltpu.make_async_copy(
+        w_ref.at[part(colour)], wbuf.at[z, part(colour)], local.at[0]
+    )
+
+    @pl.when(mine)
+    def _():
+        own_weights.start()
+
+    @pl.when(jnp.logical_not(inner))
+    def _():
+        xall[pl.ds(22 * core, RADIUS)] = jnp.zeros((RADIUS, WIDE, D), jnp.bfloat16)
+
     pl.semaphore_wait(barrier, count)
 
-    @pl.when(z > 0)
-    def _():
-        pl.semaphore_wait(token, 1)
-
-    @pl.when(z < Z - 1)
-    def _():
-        pl.semaphore_signal(
-            token, inc=1, device_id=ups[0], device_id_type=pl.DeviceIdType.MESH
-        )
+    def feed(i):
+        rows = part(x + 2 * (over + far_lo + i))
+        return remote(w_ref.at[rows], wbuf.at[z, rows], xsends.at[i], xrecvs.at[0], fed(i))
+
+    @pl.when(jnp.logical_and(mine, ends))
+    def _():
+        feed(0).start()
+        feed(1).start()
 
     def tell(semaphore, device):
         pl.semaphore_signal(
             semaphore, inc=1, device_id=device, device_id_type=pl.DeviceIdType.MESH
         )
 
+    @pl.when(jnp.logical_and(z > 0, jnp.logical_or(z % 2 == 0, z == Z - 1)))
+    def _():
+        pl.semaphore_wait(token, 1)
+
+    @pl.when(jnp.logical_and(z % 2 == 0, z < Z - 2))
+    def _():
+        tell(token, ups[1])
+
+    @pl.when(z == Z - 2)
+    def _():
+        tell(token, ups[0])
+        tell(opened, ups[1])
+
+
     @pl.when(z == Z - 1)
     def _():
         tell(opened, ups[0])
@@ -177,13 +190,9 @@
         def _():
             tell(reached, (vert, east))
 
-    @pl.when(z == Z - 2)
-    def _():
-        tell(opened, ups[1])
-
     def along(p, rows, kind, landing, device):
         ref = wbuf.at[p, rows]
-        return remote(ref, ref, sends.at[kind, p], recvs.at[landing, p], device)
+        return remote(ref, ref, sends.at[kind], recvs.at[landing, p], device)
 
     def behind(d):
         return (z + Z - d) % Z
@@ -228,17 +237,14 @@
     def pushes(p):
         kind = 2 * STRIDE
         return [
-            along(p, part(colour), kind, 2, x_up),
-            along(p, part(colour), kind + 1, 3, x_down),
-            along(p, first(colour), kind + 2, 4, y_up),
-            along(p, second(colour), kind + 3, 5, y_down),
+            along(p, part(colour), kind, 1, x_up),
+            along(p, part(colour), kind + 1, 1, x_down),
+            along(p, first(colour), kind + 2, 1, y_up),
+            along(p, second(colour), kind + 3, 1, y_down),
         ]
 
     def start(copy):
         copy.start()
-
-    def finish(copy):
-        copy.wait_send()
 
     def own_out():
         relay_up(0, start)
@@ -296,36 +302,33 @@
         lax.fori_loop(0, 3, body, 0)
 
     def drain():
-        def body(d, carry):
-            relay_up(d, finish)
-            relay_down(d, finish, False)
-            relay_down(d, finish, True)
-            for copy in pushes(behind(d)):
-                copy.wait_send()
-
-            @pl.when(jnp.logical_and(d > 0, d < 6))
+        def sent(kind, shards, rows):
+            ref = wbuf.at[pl.ds(0, shards), pl.ds(0, rows)]
+            remote(ref, ref, sends.at[kind], recvs.at[0, 0], x_up).wait_send()
+
+        sent(0, 3, PART)
+        sent(2, 3, PART)
+        for kind, third in (
+            (1, jnp.logical_and(z >= 4, z <= 9)),
+            (3, jnp.logical_and(z >= 2, z <= 7)),
+        ):
+
+            @pl.when(third)
             def _():
-                for copy in pushes(ahead(d)):
-                    copy.wait_send()
-
-            return carry
-
-        lax.fori_loop(0, 7, body, 0)
+                sent(kind, 3, PART)
+
+            @pl.when(jnp.logical_not(third))
+            def _():
+                sent(kind, 2, PART)
+
+        sent(4, Z, PART)
+        sent(5, Z, PART)
+        sent(6, Z, HALF)
+        sent(7, Z, HALF)
 
     def filled(p):
-        along(p, part(colour + 3), 0, 2, x_up).wait_recv()
-        along(p, part(colour + 1), 0, 3, x_down).wait_recv()
-        along(p, first(colour + 2), 0, 4, y_up).wait_recv()
-        along(p, second(colour + 2), 0, 5, y_down).wait_recv()
-
-    def feed(i):
-        rows = part(x + 2 * (over + far_lo + i))
-        return remote(w_ref.at[rows], wbuf.at[z, rows], xsends.at[i], xrecvs.at[0], fed(i))
-
-    @pl.when(jnp.logical_and(mine, ends))
-    def _():
-        feed(0).start()
-        feed(1).start()
+        ref = wbuf.at[p, pl.ds(0, 3 * PART)]
+        remote(ref, ref, sends.at[0], recvs.at[1, p], x_up).wait_recv()
 
     @pl.when(mine)
     def _():
@@ -481,14 +484,13 @@
     def out_copy(j, cols):
         return remote(obuf.at[j], out_ref.at[:, cols], osends.at[j], orecvs.at[j], mate)
 
-    def heads(i, carry):
-        j = (z + jnp.where(i < 2, i, 5 - i)) % 4
+    def heads(i):
+        j = (z + jnp.where(i == 0, 0, jnp.where(i == 1, 3, i - 1))) % 4
         for b in range(2):
             obuf[j, 64 * b : 64 * b + 64, :] = attend(j, 2 * (1 - core) + b)
         out_copy(j, block(j)).start()
         for b in range(2):
             out_ref[64 * b : 64 * b + 64, block(j)] = attend(j, 2 * core + b)
-        return carry
 
     def tokens_in():
         for copy in halo_copies(0, 1):
@@ -525,8 +527,17 @@
 
         lax.fori_loop(low, high, body, 0)
 
-    def attend_pairs(low, high):
-        lax.fori_loop(low, high, heads, 0)
+    def finish_pairs():
+        def shard(i, carry):
+            consume(i, True)
+            return carry
+
+        def body(k, carry):
+            lax.fori_loop(jnp.where(k == 0, 1, 8 + k), 9 + k, shard, 0)
+            heads(k)
+            return carry
+
+        lax.fori_loop(0, 4, body, 0)
 
     early_shards()
     open_wrap()
@@ -537,8 +548,7 @@
     project_shards(0, 5, False)
     late_shards(4, 6)
     project_shards(5, 11, False)
-    project_shards(1, 12, True)
-    attend_pairs(0, 4)
+    finish_pairs()
 
     drain()
 
@@ -582,8 +592,8 @@
             pltpu.VMEM((4, 128, 512), jnp.float32),
             pltpu.VMEM((2, 2, TILE, 20 * WIDE), jnp.float32),
             pltpu.VMEM((4, 128, 128), jnp.bfloat16),
-            dma((2 * STRIDE + 4, Z)),
-            dma((6, Z)),
+            dma((2 * STRIDE + 4,)),
+            dma((2, Z)),
             dma((2,)),
             dma((1,)),
             dma((7,)),

time: 60.1 us -> 56.7 us (0.943)
  the two profiles are of different devices: /device:TPU:497 before, /device:TPU:1 now
where the time goes in v4:
time: 56.7 us; the launch traced here: 56.5 us
  Pallas kernels  54.8 us (97%)
  local copies, waits for them, and re-layouts  1.67 us (3%)
    pallas_call x1, Pallas kernels, per_device(): pl.pallas_call(kernel, out_shape=jax.ShapeDtypeStruct((rows * cols, width...  54.8 us
    unnamed x1, local copies, waits for them, and re-layouts  1.67 us

profile of v4, /device:TPU:1, one launch (start us, length us, event | category | flops | bytes accessed | tf_op | source)
XLA Modules:
  0.0 56.5 jit_solution(10228967475210815327)
XLA Ops:
  0.0 54.8 %shard_map.46 = bf16[128,1024]{1,0:T(8,128)(2,1)} custom-call(bf16[8,16,1024]{2,1,0:T(8,128)(2,1)} %tok_ref.1, bf16[1024,128]{1,0:T(8,128)(2,1)} %w_ref.1, f32[13,16,13]{2,1,0:T(8,128)} %bitcast.3, s32[1,2,9]{2,1,0:T(2,128)} %flag_ref.1), custom_call_target="tpu_custom_call" | custom-call | tf_op jit(solution)/shard_map/pallas_call | solution.py:581
  54.8 1.7 %copy.6 = bf16[8,16,1024]{2,1,0:T(8,128)(2,1)} copy(bf16[8,16,1024]{2,1,0:T(8,128)(2,1)} %bitcast.2) | data formatting | bytes 524288

commit v5 on v4

--- a/solution.py
+++ b/solution.py
@@ -22,6 +22,7 @@
 Y = 8
 Z = 12
 STRIDE = 2
+FAR = 7
 PART = D // 4
 HALF = PART // 2
 
@@ -94,7 +95,10 @@
         return place(x, over + far_lo + i, z)
 
     middle = jnp.where(z // 4 == 1, 1, 0)
-    mine = yhi == (core + middle) % 2
+    owner = (core + middle) % 2
+    mine = yhi == owner
+    up_lacks = ((y + 1) % Y) // 4 != owner
+    down_lacks = ((y + Y - 1) % Y) // 4 != owner
 
     def part(c):
         return pl.ds(pl.multiple_of((c % 4) * PART, PART), PART)
@@ -139,7 +143,7 @@
     own_tokens = pltpu.make_async_copy(tok_ref, xall.at[pl.ds(mid, 8), 8:24], local.at[1])
     own_tokens.start()
     own_weights = pltpu.make_async_copy(
-        w_ref.at[part(colour)], wbuf.at[z, part(colour)], local.at[0]
+        w_ref, wbuf.at[z], local.at[0]
     )
 
     @pl.when(mine)
@@ -200,39 +204,28 @@
     def ahead(d):
         return (z + d) % Z
 
-    def relay_up(d, act):
-        p = behind(d)
-
-        @pl.when(jnp.logical_and(d % STRIDE == 0, d < 6))
-        def _():
-            act(along(p, part(colour), 0, 0, ups[0]))
-
-            @pl.when(d < 4)
+    def goes_up(d, i):
+        inside = jnp.logical_and(d <= z, z + i < Z)
+        return jnp.logical_and(d % STRIDE == 0, d + i <= jnp.where(inside, FAR, 5))
+
+    def goes_down(d, i):
+        inside = jnp.logical_and(z + d < Z, z >= i)
+        return jnp.logical_and(d % STRIDE == 0, d + i <= jnp.where(inside, 6, 11 - FAR))
+
+    def relay_up(d):
+        for i in (1, 2):
+
+            @pl.when(goes_up(d, i))
             def _():
-                act(along(p, part(colour), 1, 0, ups[1]))
-
-            @pl.when(jnp.logical_and(d == 4, p < 6))
+                along(behind(d), part(colour), i - 1, 0, ups[i - 1]).start()
+
+    def relay_down(d, crossing):
+        for i in (1, 2):
+            here = (z < i) if crossing else (z >= i)
+
+            @pl.when(jnp.logical_and(here, goes_down(d, i)))
             def _():
-                act(along(p, part(colour), 1, 0, ups[1]))
-
-    def relay_down(d, act, crossing):
-        p = ahead(d)
-        for i in range(STRIDE):
-            here = (z < i + 1) if crossing else (z >= i + 1)
-
-            @pl.when(jnp.logical_and(here, jnp.logical_and(d % STRIDE == 0, d < 6)))
-            def _():
-                if i == 0:
-                    act(along(p, part(colour), 2, 0, downs[0]))
-                else:
-
-                    @pl.when(d < 4)
-                    def _():
-                        act(along(p, part(colour), 3, 0, downs[1]))
-
-                    @pl.when(jnp.logical_and(d == 4, p >= 6))
-                    def _():
-                        act(along(p, part(colour), 3, 0, downs[1]))
+                along(ahead(d), part(colour), i + 1, 0, downs[i - 1]).start()
 
     def pushes(p):
         kind = 2 * STRIDE
@@ -243,49 +236,63 @@
             along(p, second(colour), kind + 3, 1, y_down),
         ]
 
-    def start(copy):
-        copy.start()
-
     def own_out():
-        relay_up(0, start)
-        relay_down(0, start, False)
-        for copy in pushes(z):
-            copy.start()
+        relay_up(0)
+        relay_down(0, False)
+        own = pushes(z)
+
+        @pl.when(jnp.logical_not(mine))
+        def _():
+            own[0].start()
+            own[1].start()
+
+        @pl.when(up_lacks)
+        def _():
+            own[2].start()
+
+        @pl.when(down_lacks)
+        def _():
+            own[3].start()
 
     def whole_in(p):
         along(p, part(colour), 0, 0, ups[0]).wait_recv()
 
+    def from_low(d, late):
+        if late:
+            return jnp.logical_and(d > z, d < 6)
+        return jnp.logical_and(d <= z, d <= FAR)
+
+    def from_high(d, late):
+        crossed = jnp.logical_and(z + d >= Z, d <= 11 - FAR)
+        if late:
+            return jnp.logical_or(crossed, jnp.logical_and(d == 6, z < 6))
+        return jnp.logical_and(z + d < Z, d < 6)
+
     def pass_on(i, late):
-        d = jnp.where(i < 4, i + 2 - 2 * (i % 2), i + 1)
-
-        @pl.when(jnp.logical_and(d < 6, (d > z) == late))
+        d = jnp.where(i == 4, 5, jnp.where(i == 5, 6, i + 2 - 2 * (i % 2))) if late else (
+            i + 2 - 2 * (i % 2)
+        )
+
+        @pl.when(from_low(d, late))
         def _():
             whole_in(behind(d))
-            relay_up(d, start)
+            relay_up(d)
             for copy in pushes(behind(d)):
                 copy.start()
 
-        @pl.when(jnp.logical_and(d < 6, (z + d >= Z) == late))
+        @pl.when(from_high(d, late))
         def _():
             whole_in(ahead(d))
-            relay_down(d, start, False)
+            relay_down(d, False)
             for copy in pushes(ahead(d)):
                 copy.start()
-
-        if late:
-
-            @pl.when(d == 6)
-            def _():
-                whole_in(behind(d))
-                for copy in pushes(behind(d)):
-                    copy.start()
 
     def early_shards():
         def body(i, carry):
             pass_on(i, False)
             return carry
 
-        lax.fori_loop(0, 5, body, 0)
+        lax.fori_loop(0, FAR + FAR % 2, body, 0)
 
     def late_shards(low, high):
         def body(i, carry):
@@ -296,7 +303,7 @@
 
     def cross_down():
         def body(i, carry):
-            relay_down(2 * i, start, True)
+            relay_down(2 * i, True)
             return carry
 
         lax.fori_loop(0, 3, body, 0)
@@ -306,25 +313,31 @@
             ref = wbuf.at[pl.ds(0, shards), pl.ds(0, rows)]
             remote(ref, ref, sends.at[kind], recvs.at[0, 0], x_up).wait_send()
 
-        sent(0, 3, PART)
-        sent(2, 3, PART)
-        for kind, third in (
-            (1, jnp.logical_and(z >= 4, z <= 9)),
-            (3, jnp.logical_and(z >= 2, z <= 7)),
+        for kind, goes, i in ((0, goes_up, 1), (1, goes_up, 2), (2, goes_down, 1), (3, goes_down, 2)):
+            number = 0
+            for d in (0, 2, 4, 6, 8):
+                number = number + jnp.where(goes(d, i), 1, 0)
+            for n in range(1, 6):
+
+                @pl.when(number == n)
+                def _():
+                    sent(kind, n, PART)
+
+        lacks = jnp.logical_not(mine)
+        for kind, some, rows in (
+            (4, lacks, PART),
+            (5, lacks, PART),
+            (6, up_lacks, HALF),
+            (7, down_lacks, HALF),
         ):
 
-            @pl.when(third)
+            @pl.when(some)
             def _():
-                sent(kind, 3, PART)
-
-            @pl.when(jnp.logical_not(third))
+                sent(kind, Z, rows)
+
+            @pl.when(jnp.logical_not(some))
             def _():
-                sent(kind, 2, PART)
-
-        sent(4, Z, PART)
-        sent(5, Z, PART)
-        sent(6, Z, HALF)
-        sent(7, Z, HALF)
+                sent(kind, Z - 1, rows)
 
     def filled(p):
         ref = wbuf.at[p, pl.ds(0, 3 * PART)]
@@ -450,11 +463,13 @@
     def consume(i, late):
         d = (i + 1) // 2
         p = jnp.where(i % 2 == 1, behind(d), ahead(d))
-        far = jnp.where(i % 2 == 1, d > z, z + d >= Z)
-
-        @pl.when(jnp.logical_or(far, d == 6) == late)
-        def _():
-            filled(p)
+
+        @pl.when(jnp.where(i % 2 == 1, from_low(d, late), from_high(d, late)))
+        def _():
+            @pl.when(jnp.logical_not(jnp.logical_and(mine, p == z)))
+            def _():
+                filled(p)
+
             project(p)
 
     small = lax.broadcasted_iota(jnp.int32, (64, 128), 1)
@@ -533,7 +548,8 @@
             return carry
 
         def body(k, carry):
-            lax.fori_loop(jnp.where(k == 0, 1, 8 + k), 9 + k, shard, 0)
+            low = jnp.where(k == 0, 1, 8 + k)
+            lax.fori_loop(low, 9 + k + k // 3, shard, 0)
             heads(k)
             return carry
 
@@ -547,7 +563,7 @@
     region_in()
     project_shards(0, 5, False)
     late_shards(4, 6)
-    project_shards(5, 11, False)
+    project_shards(5, 2 * FAR, False)
     finish_pairs()
 
     drain()

time: 56.7 us -> 56.5 us (level)
  no operation moved by 1% of the time
where the time goes in v5:
time: 56.5 us; the launch traced here: 56 us
  Pallas kernels  54.3 us (96%)
  local copies, waits for them, and re-layouts  1.67 us (3%)
    pallas_call x1, Pallas kernels, per_device(): pl.pallas_call(kernel, out_shape=jax.ShapeDtypeStruct((rows * cols, width...  54.3 us
    unnamed x1, local copies, waits for them, and re-layouts  1.67 us

profile of v5, /device:TPU:1, one launch (start us, length us, event | category | flops | bytes accessed | tf_op | source)
XLA Modules:
  0.0 56.0 jit_solution(3609625677107952442)
XLA Ops:
  0.0 54.3 %shard_map.46 = bf16[128,1024]{1,0:T(8,128)(2,1)} custom-call(bf16[8,16,1024]{2,1,0:T(8,128)(2,1)} %tok_ref.1, bf16[1024,128]{1,0:T(8,128)(2,1)} %w_ref.1, f32[13,16,13]{2,1,0:T(8,128)} %bitcast.3, s32[1,2,9]{2,1,0:T(2,128)} %flag_ref.1), custom_call_target="tpu_custom_call" | custom-call | tf_op jit(solution)/shard_map/pallas_call | solution.py:597
  54.3 1.7 %copy.6 = bf16[8,16,1024]{2,1,0:T(8,128)(2,1)} copy(bf16[8,16,1024]{2,1,0:T(8,128)(2,1)} %bitcast.2) | data formatting | bytes 524288
